TPU v7x, 32 devices: a whole 2x2x4 slice. The times are simulated.
32 devices in a mesh: ctx: 8 (over y, x, core), head: 4 (over z).
Axes of the slice: x: 2, y: 2, z: 4, core: 2. Of those that a mesh axis runs over, the one named last changes fastest.
Arguments:
- queries: bfloat16 [4096, 4096], P(('ctx', 'head')), may hold values from -128 to 128
- vis_feats: bfloat16 [4096, 8192], P('ctx', 'head'), may hold values from -16 to 16
- kv_weight: bfloat16 [8192, 1024], P('head'), may hold values from -0.044194174 to 0.044194174
- key_gain: float32 [128], replicated, may hold values from 0.1 to 1.9
- cross_mask: int32 [4096, 4], P('ctx'), may hold values 0 or 1
- image_tokens: int32 [4], replicated, may hold values from 1 to 512, 1280 in all
- image_owner: int32 [4], replicated, may hold values from 0 to 7, as said below
Outputs:
- attended: bfloat16 [4096, 4096], P(('ctx', 'head'))
Inputs may be any that keep to these rules, and one draw needn't show every extreme that they name: `image_tokens`: they sum to 1280; the largest is exactly 512. `image_owner`: four distinct context indices; the first and the last index of ctx always hold an image.
All inputs are finite; a program needn't handle non-finite values. No bound on the sum of `cross_mask` on one device may be relied on, other than what follows from the above.
Results may differ from a plain program's by a relative error of at most 0.0014.
The roundings to bfloat16 on the way count: a program that leaves them out, or rounds other values in their place, can miss the bound.
Values may be sent and summed in bfloat16 or wider, within the bound.
No kernel may reach another device: no remote copies, remote signals or barrier semaphores. Data moves between devices by JAX's collectives and lax.ppermute only.
A program may use at most 64 MiB of HBM per device.

v0:
```python
import jax
import jax.numpy as jnp
from jax import lax
from jax.sharding import PartitionSpec as P

EPSILON = 1e-05
FLOOR_SCORE = -1e30


def swapped(value, axis, bit):
    mask = 2**bit
    pairs = [(source, source ^ mask) for source in range(lax.axis_size(axis))]
    return lax.ppermute(value, axis, pairs)


def broadcast(shard, axis, root):
    mine = lax.axis_index(axis) == root
    return lax.psum(jnp.where(mine, shard, jnp.zeros_like(shard)), axis)


def normalize_keys(stacked, key_gain):
    raw_keys = stacked[..., 0, :, :]
    square_mean = jnp.mean(raw_keys * raw_keys, axis=-2, keepdims=True)
    normed = raw_keys * lax.rsqrt(square_mean + EPSILON) * key_gain[:, None]
    joined = jnp.stack([normed, stacked[..., 1, :, :]], axis=-3)
    return joined.astype(jnp.bfloat16)


def arrange_keys(received, image_tokens):
    cap_rows = received[0].shape[-1]
    count_img = len(received)
    img_ids = jnp.arange(count_img, dtype=jnp.int32)
    laid_out = jnp.concatenate(received, axis=-1)
    positions = jnp.arange(count_img * cap_rows, dtype=jnp.int32)[:, None]
    member = (positions // cap_rows == img_ids[None, :]) & (
        positions % cap_rows < image_tokens[None, :]
    )
    return (laid_out, member.astype(jnp.float32))


def attend_rows(query_rows, mask_rows, key_cols, value_cols, member):
    row_count = query_rows.shape[0]
    rows_per_block = min(512, row_count)
    count_of_blocks = row_count // rows_per_block
    blocked_queries = query_rows.reshape((count_of_blocks, rows_per_block) + query_rows.shape[1:])
    mask_blocks = mask_rows.reshape(count_of_blocks, rows_per_block, mask_rows.shape[1])
    factor = query_rows.shape[-1] ** (-0.5)
    member_rows = member.T

    def one_block(block_pair):
        query_block, mask_block = block_pair
        allowed = jnp.dot(mask_block.astype(jnp.float32), member_rows) > 0.5
        allowed = allowed[:, None, :]
        scores = (
            jnp.einsum("rnd,dk->rnk", query_block, key_cols, preferred_element_type=jnp.float32)
            * factor
        )
        largest = jnp.max(jnp.where(allowed, scores, FLOOR_SCORE), axis=-1, keepdims=True)
        weights = jnp.where(allowed, jnp.exp(scores - largest), 0.0)
        summed = jnp.sum(weights, axis=-1, keepdims=True)
        mixed_out = jnp.einsum(
            "rnk,dk->rnd",
            weights.astype(jnp.bfloat16),
            value_cols,
            preferred_element_type=jnp.float32,
        )
        return (mixed_out / jnp.maximum(summed, 1.0)).astype(jnp.bfloat16)

    return lax.map(one_block, (blocked_queries, mask_blocks)).reshape(query_rows.shape)


def shards(queries, vis_feats, kv_weight, key_gain, cross_mask, image_tokens, image_owner):
    head_count = lax.axis_size("head")
    head_index = lax.axis_index("head")
    count_img = image_owner.shape[0]
    width_kv = kv_weight.shape[1]
    head_dim = key_gain.shape[0]
    kv_heads = width_kv // (2 * head_dim)
    tok_rows = queries.shape[0]
    query_heads = queries.shape[1] // head_dim
    per_kv = head_count // kv_heads
    share_part = lax.psum_scatter(
        lax.dot_general(
            kv_weight, vis_feats, (((0,), (1,)), ((), ())), preferred_element_type=jnp.float32
        ),
        "head",
        scatter_dimension=0,
        tiled=True,
    )
    for bit_index in range(per_kv.bit_length() - 1):
        partner = swapped(share_part, "head", bit_index)
        low_half = (head_index >> bit_index) % 2 == 0
        share_part = jnp.where(
            low_half,
            jnp.concatenate([share_part, partner], 0),
            jnp.concatenate([partner, share_part], 0),
        )
    local_kv = normalize_keys(share_part.reshape(1, 2, head_dim, -1), key_gain)[0].reshape(
        2 * head_dim, -1
    )
    received = [
        broadcast(local_kv, "ctx", image_owner[img_index]) for img_index in range(count_img)
    ]
    laid_out, member = arrange_keys(received, image_tokens)
    key_cols = laid_out[:head_dim]
    value_cols = laid_out[head_dim:]
    group_size = query_heads // head_count
    grouped = queries.reshape(tok_rows, head_count, group_size, head_dim)
    exchanged = lax.all_to_all(grouped, "head", split_axis=1, concat_axis=0, tiled=True)
    rows_all = exchanged.shape[0]
    flat_rows = exchanged.reshape(rows_all, exchanged.shape[2], head_dim)
    attended_heads = attend_rows(flat_rows, cross_mask, key_cols, value_cols, member).reshape(
        exchanged.shape
    )
    restored = lax.all_to_all(attended_heads, "head", split_axis=0, concat_axis=1, tiled=True)
    return restored.reshape(tok_rows, query_heads * head_dim)


def solution(mesh):
    return jax.shard_map(
        shards,
        mesh=mesh,
        in_specs=(
            P(("ctx", "head"), None),
            P("ctx", "head"),
            P("head", None),
            P(),
            P("ctx", None),
            P(),
            P(),
        ),
        out_specs=P(("ctx", "head"), None),
        check_vma=False,
    )
```

profile of v0, /device:TPU:0, one launch (start us, length us, event | category | flops | bytes accessed | tf_op | source)
XLA Modules:
  0.0 219.0 jit_solution(8036381709302970630)
XLA Ops:
  6.5 0.0 copy-start
  6.5 0.0 copy-start.1
  6.5 0.0 copy-start.2
  6.5 0.0 copy-start.4
  6.5 0.0 copy-start.3
  6.5 0.0 reduce-scatter.2.cloned.1.call-start
  6.6 1.5 copy-done
  8.1 5.9 %fusion.36 = f32[1024,512]{1,0:T(8,128)} fusion(bf16[2048,1024]{1,0:T(8,128)(2,1)} %param.9, bf16[512,2048]{1,0:T(8,128)(2,1)S(1)} %copy-done), kind=kOutput, calls=%fused_computation.55 | convolution fusion | flops 2147483648 | bytes 8388608 | tf_op jit(solution)/shard_map/dot_general | solution.py:83
  14.0 0.0 reduce-scatter.2.cloned.1.call-update
  14.0 1.6 copy.29
  15.7 1.3 copy.30
  17.0 6.3 %all-to-all-start = ((bf16[128,4,8,128]{3,0,2,1:T(8,128)(2,1)}), bf16[128,4,8,128]{3,0,2,1:T(8,128)(2,1)S(1)}, u32[]{:S(2)}, u32[]{:S(2)}) async-start(bf16[128,4,8,128]{3,0,2,1:T(8,128)(2,1)} %copy.30), calls=%async_computation.1 | async-start | bytes 2097152 | tf_op jit(solution)/shard_map/all_to_all | solution.py:109
  23.3 0.0 all-reduce.3.cloned.1.call-start
  23.3 0.0 copy-done.1
  23.4 0.7 fusion.34
  26.5 54.1 %reduce-scatter.2.cloned.1.call-done = f32[256,512]{1,0:T(8,128)} async-done(((f32[1024,512]{1,0:T(8,128)}), f32[256,512]{1,0:T(8,128)}) %reduce-scatter.2.cloned.1.call-update) | async-done | bytes 524304 | tf_op jit(solution)/shard_map/reduce_scatter | solution.py:82
  80.5 1.0 slice.49
  81.5 1.0 multiply_reduce_fusion
  82.5 0.0 copy-done.2
  82.5 1.0 multiply_convert_fusion
  83.6 0.9 broadcast_select_fusion
  84.5 1.8 copy.41
  86.3 1.8 copy.39
  88.0 1.8 copy.40
  89.8 0.8 copy.38
  90.7 0.0 all-reduce.3.cloned.1.call-update
  90.7 0.0 copy-done.4
  90.7 0.0 copy-done.3
  90.7 2.6 %compare_bitcast_fusion = pred[512,2048]{0,1:T(8,128)(4,1)} fusion(s32[4]{0:T(128)S(1)} %copy-done.4, s32[2048]{0:T(1024)S(1)} %get-tuple-element.41, s32[2048]{0:T(1024)S(1)} %get-tuple-element.40, s32[512,4]{0,1:T(4,128)S(1)} %copy-done.3), kind=kOutput, calls=%fused_computation.12 | convolution fusion | flops 9463808 | bytes 1073168 | tf_op jit(solution)/shard_map/while/body/eval_jaxpr/dot_general | solution.py:52
  93.3 0.0 all-to-all-done
  93.3 1.1 copy.31
  94.4 54.2 %all-reduce.3.cloned.1.call-done = (bf16[256,512]{0,1:T(8,128)(2,1)}, bf16[256,512]{0,1:T(8,128)(2,1)}, bf16[256,512]{0,1:T(8,128)(2,1)}, bf16[256,512]{0,1:T(8,128)(2,1)}) async-done(((bf16[256,512]{0,1:T(8,128)(2,1)}, bf16[256,512]{0,1:T(8,128)(2,1)}, bf16[256,512]{0,1:T(8,128)(2,1)}, bf16[256,512]{0,1:T(8,128)(2,1)}), (bf16[256,512]{0,1:T(8,128)(2,1)}, bf16[256,512]{0,1:T(8,128)(2,1)}, ...) | async-done | bytes 1048592 | tf_op jit(solution)/shard_map/psum | solution.py:18
  148.5 1.0 constant_dynamic-update-slice_fusion.3
  149.5 1.0 constant_dynamic-update-slice_fusion.2
  150.5 1.0 constant_dynamic-update-slice_fusion.1
  151.4 1.0 constant_dynamic-update-slice_fusion
  152.4 17.6 %fusion.35 = (f32[512,8]{0,1:T(8,128)S(1)}, bf16[512,8,2048]{0,2,1:T(8,128)(2,1)}) fusion(pred[512,2048]{0,1:T(8,128)(4,1)} %compare_bitcast_fusion, bf16[512,8,128]{2,0,1:T(8,128)(2,1)} %bitcast.66, bf16[256,2048]{0,1:T(8,128)(2,1)S(1)} %constant_dynamic-update-slice_fusion), kind=kOutput, calls=%fused_computation.54 | convolution fusion | flops 4353689600 | bytes 22036480 | tf_op jit(solution)/shard_map/while/body/eval_jaxpr/sub | solution.py:59
  170.0 10.8 %fusion.14 = bf16[512,1,8,128]{3,0,2,1:T(8,128)(2,1)S(1)} fusion(bf16[512,8,2048]{0,2,1:T(8,128)(2,1)} %get-tuple-element.39, f32[512,8]{0,1:T(8,128)S(1)} %broadcast_maximum_fusion, bf16[256,2048]{0,1:T(8,128)(2,1)S(1)} %constant_dynamic-update-slice_fusion), kind=kOutput, calls=%fused_computation.15 | convolution fusion | flops 2148532224 | bytes 18366464 | tf_op jit(solution)/shard_map/while/body/eval_jaxpr/rnk,dk->rnd/dot_general | solution.py:61
  180.8 0.7 copy.34
  181.5 29.3 %all_to_all.30 = bf16[512,1,8,128]{3,2,1,0:T(8,128)(2,1)S(1)} all-to-all(bf16[512,1,8,128]{3,2,1,0:T(8,128)(2,1)S(1)} %copy.34), channel_id=1, replica_groups=mesh['ctx'=8,'head'=4] {'head'}, dimensions={0} | all-to-all | bytes 2097152 | tf_op jit(solution)/shard_map/all_to_all | solution.py:115
  210.7 0.2 copy.35
  210.9 1.3 reshape.149
  (3 shorter events, 0.0 us)
Async XLA Ops:
  6.5 1.6 copy-start
  6.5 16.8 %copy-start.1 = (s32[4]{0:T(128)S(1)}, s32[4]{0:T(128)}, u32[]{:S(2)}) copy-start(s32[4]{0:T(128)} %param.13) | copy-start | bytes 52
  6.5 76.0 %copy-start.2 = (f32[128]{0:T(128)S(1)}, f32[128]{0:T(128)}, u32[]{:S(2)}) copy-start(f32[128]{0:T(128)} %param.10) | copy-start | bytes 1540
  6.5 84.2 %copy-start.4 = (s32[4]{0:T(128)S(1)}, s32[4]{0:T(128)}, u32[]{:S(2)}) copy-start(s32[4]{0:T(128)} %param.12) | copy-start | bytes 52
  6.5 84.2 %copy-start.3 = (s32[512,4]{0,1:T(4,128)S(1)}, s32[512,4]{0,1:T(4,128)}, u32[]{:S(2)}) copy-start(s32[512,4]{0,1:T(4,128)} %param.11) | copy-start | bytes 24580
  6.5 74.0 %reduce-scatter.2.cloned.1.call-start = ((), (), s32[]{:S(2)}) async-start(), calls=%async_computation.3 | async-start | bytes 2621440 | tf_op jit(solution)/shard_map/reduce_scatter | solution.py:82
  17.0 76.3 %all-to-all-start = ((bf16[128,4,8,128]{3,0,2,1:T(8,128)(2,1)}), bf16[128,4,8,128]{3,0,2,1:T(8,128)(2,1)S(1)}, u32[]{:S(2)}, u32[]{:S(2)}) async-start(bf16[128,4,8,128]{3,0,2,1:T(8,128)(2,1)} %copy.30), calls=%async_computation.1 | async-start | bytes 2097152 | tf_op jit(solution)/shard_map/all_to_all | solution.py:109
  23.3 125.2 %all-reduce.3.cloned.1.call-start = ((), (), s32[]{:S(2)}) async-start(), calls=%async_computation.4 | async-start | bytes 2097152 | tf_op jit(solution)/shard_map/psum | solution.py:18
Sparse Core Ops, SparseCore 0:
  14.2 66.3 reduce-scatter.1
  90.8 57.6 all-reduce.2
where the time goes:
time: 220 us; the launch traced here: 219 us
  waiting for transfers between devices  108 us (49%)
  matrix products  36.8 us (17%)
  blocking collectives  29.3 us (13%)
  local copies, waits for them, and re-layouts  19.4 us (9%)
  between operations  16 us (7%)
  starting transfers between devices  6.38 us (3%)
  other arithmetic  2.95 us (1%)
    psum x1, waiting for transfers between devices, broadcast(): return lax.psum(jnp.where(mine, shard, jnp.zeros_like(shard)), axis)  54.2 us
    reduce_scatter x1, waiting for transfers between devices, shards(): lax.psum_scatter(lax.dot_general(kv_weight, vis_feats, (((0,), (1,)), (()...  54.1 us
    all_to_all x1, blocking collectives, shards(): lax.all_to_all(attended_heads, 'head', split_axis=0, concat_axis=1, tiled...  29.3 us
    sub x1, matrix products, one_block(): weights = jnp.where(allowed, jnp.exp(scores - largest), 0.0)  17.6 us
    dot_general x1, matrix products, one_block(): jnp.einsum('rnk,dk->rnd', weights.astype(jnp.bfloat16), value_cols, prefe...  10.8 us
    all_to_all x1, starting transfers between devices, shards(): lax.all_to_all(grouped, 'head', split_axis=1, concat_axis=0, tiled=True)  6.34 us
    select_n x4, local copies, waits for them, and re-layouts, broadcast(): return lax.psum(jnp.where(mine, shard, jnp.zeros_like(shard)), axis)  6.19 us
    unnamed x14, local copies, waits for them, and re-layouts  6.07 us
  transfers between devices with their start and end apart: 3, of which 2 were waited for; matrix products, arithmetic and copies ran while one was open for 8% of the time, Pallas kernels for 0%

commit v1 on v0

--- a/solution.py
+++ b/solution.py
@@ -15,7 +15,7 @@
 
 def broadcast(shard, axis, root):
     mine = lax.axis_index(axis) == root
-    return lax.psum(jnp.where(mine, shard, jnp.zeros_like(shard)), axis)
+    return jnp.sum(lax.all_gather(jnp.where(mine, shard, jnp.zeros_like(shard)), axis), axis=0)
 
 
 def normalize_keys(stacked, key_gain):

time: 220 us -> 255 us (1.16)
  waiting for transfers between devices: 108 us -> 140 us
  other arithmetic: 2.95 us -> 13.2 us
  local copies, waits for them, and re-layouts: 19.4 us -> 12.9 us
    all_gather x0 -> x4, waiting for transfers between devices: none -> 72.3 us  [broadcast(): lax.all_gather(jnp.where(mine, shard, jnp.zeros_like(shard)), axis)]
    psum x1 -> x0, waiting for transfers between devices: 54.2 us -> none  [broadcast(): return lax.psum(jnp.where(mine, shard, jnp.zeros_like(shard)), axis)]
    all_to_all x1, waiting for transfers between devices: 0.01 us -> 22.8 us  [shards(): lax.all_to_all(grouped, 'head', split_axis=1, concat_axis=0, tiled=True)]
    reduce_scatter x1, waiting for transfers between devices: 54.1 us -> 43.1 us  [shards(): lax.psum_scatter(lax.dot_general(kv_weight, vis_feats, (((0,), (1,)), (()...]
    reduce_sum x0 -> x4, other arithmetic: none -> 7.93 us  [broadcast(): jnp.sum(lax.all_gather(jnp.where(mine, shard, jnp.zeros_like(shard)), axi...]
    select_n x4 -> x0, local copies, waits for them, and re-layouts: 6.19 us -> none  [broadcast(): return lax.psum(jnp.where(mine, shard, jnp.zeros_like(shard)), axis)]
    reduce_sum x0 -> x4, local copies, waits for them, and re-layouts: none -> 3.4 us  [broadcast(): jnp.sum(lax.all_gather(jnp.where(mine, shard, jnp.zeros_like(shard)), axi...]
    unnamed x14 -> x13, local copies, waits for them, and re-layouts: 6.07 us -> 3.22 us
  transfers between devices with their start and end apart: 3 -> 6, of which waited for: 2 -> 5; matrix products, arithmetic and copies ran while one was open for 8% -> 6% of each run, Pallas kernels for 0% -> 0%
where the time goes in v1:
time: 255 us; the launch traced here: 254 us
  waiting for transfers between devices  140 us (55%)
  matrix products  37.5 us (15%)
  blocking collectives  30.5 us (12%)
  between operations  16 us (6%)
  other arithmetic  13.2 us (5%)
  local copies, waits for them, and re-layouts  12.9 us (5%)
  starting transfers between devices  3.87 us (2%)
    all_gather x4, waiting for transfers between devices, broadcast(): lax.all_gather(jnp.where(mine, shard, jnp.zeros_like(shard)), axis)  72.3 us
    reduce_scatter x1, waiting for transfers between devices, shards(): lax.psum_scatter(lax.dot_general(kv_weight, vis_feats, (((0,), (1,)), (()...  43.1 us
    all_to_all x1, blocking collectives, shards(): lax.all_to_all(attended_heads, 'head', split_axis=0, concat_axis=1, tiled...  30.5 us
    all_to_all x1, waiting for transfers between devices, shards(): lax.all_to_all(grouped, 'head', split_axis=1, concat_axis=0, tiled=True)  22.8 us
    sub x1, matrix products, one_block(): weights = jnp.where(allowed, jnp.exp(scores - largest), 0.0)  18.3 us
    dot_general x1, matrix products, one_block(): jnp.einsum('rnk,dk->rnd', weights.astype(jnp.bfloat16), value_cols, prefe...  10.8 us
    reduce_sum x4, other arithmetic, broadcast(): jnp.sum(lax.all_gather(jnp.where(mine, shard, jnp.zeros_like(shard)), axi...  7.93 us
    dot_general x1, matrix products, shards(): lax.dot_general(kv_weight, vis_feats, (((0,), (1,)), ((), ())), preferred...  5.9 us
  transfers between devices with their start and end apart: 6, of which 5 were waited for; matrix products, arithmetic and copies ran while one was open for 6% of the time, Pallas kernels for 0%

profile of v1, /device:TPU:0, one launch (start us, length us, event | category | flops | bytes accessed | tf_op | source)
XLA Modules:
  0.0 253.9 jit_solution(561631422016239301)
XLA Ops:
  6.5 0.0 copy-start
  6.5 0.0 reduce-scatter.2.cloned.1.call-start
  6.5 1.6 copy-done
  8.1 5.9 %fusion.36 = f32[1024,512]{1,0:T(8,128)} fusion(bf16[2048,1024]{1,0:T(8,128)(2,1)} %param.9, bf16[512,2048]{1,0:T(8,128)(2,1)S(1)} %copy-done), kind=kOutput, calls=%fused_computation.52 | convolution fusion | flops 2147483648 | bytes 8388608 | tf_op jit(solution)/shard_map/dot_general | solution.py:83
  14.0 0.0 reduce-scatter.2.cloned.1.call-update
  14.1 0.0 all-gather.7.cloned.1.call-start
  14.1 0.0 copy-done.2
  14.1 0.7 fusion.34
  17.5 43.1 %reduce-scatter.2.cloned.1.call-done = f32[256,512]{1,0:T(8,128)} async-done(((f32[1024,512]{1,0:T(8,128)}), f32[256,512]{1,0:T(8,128)}) %reduce-scatter.2.cloned.1.call-update) | async-done | bytes 524304 | tf_op jit(solution)/shard_map/reduce_scatter | solution.py:82
  60.6 1.0 multiply_reduce_fusion
  61.5 1.0 slice.49
  62.5 0.0 copy-done.3
  62.5 1.0 multiply_convert_fusion
  63.6 0.0 copy-start.4
  63.6 0.0 copy-start.5
  63.6 1.0 broadcast_select_fusion.3
  64.6 0.0 all-gather.7.cloned.1.call-update
  64.6 0.0 all-gather.5.cloned.1.call-start
  64.7 0.7 all-gather.5.cloned.1.call-update
  65.4 0.0 all-gather.9.cloned.1.call-start
  65.4 0.5 all-gather.9.cloned.1.call-update
  65.9 0.0 all-gather.11.cloned.1.call-start
  66.0 0.5 all-gather.11.cloned.1.call-update
  66.5 1.6 copy.25
  68.1 1.4 copy.26
  69.5 3.7 %all-to-all-start = ((bf16[128,4,8,128]{3,0,2,1:T(8,128)(2,1)}), bf16[128,4,8,128]{3,0,2,1:T(8,128)(2,1)S(1)}, u32[]{:S(2)}, u32[]{:S(2)}) async-start(bf16[128,4,8,128]{3,0,2,1:T(8,128)(2,1)} %copy.26), calls=%async_computation.1 | async-start | bytes 2097152 | tf_op jit(solution)/shard_map/all_to_all | solution.py:109
  73.2 0.0 copy-done.4
  73.3 2.6 %compare_bitcast_fusion = pred[512,2048]{0,1:T(8,128)(4,1)} fusion(s32[4]{0:T(128)S(1)} %copy-done.5, s32[2048]{0:T(1024)S(1)} %get-tuple-element.37, s32[2048]{0:T(1024)S(1)} %get-tuple-element.36, s32[512,4]{0,1:T(4,128)S(1)} %copy-done.4), kind=kOutput, calls=%fused_computation.12 | convolution fusion | flops 9463808 | bytes 1073168 | tf_op jit(solution)/shard_map/while/body/eval_jaxpr/dot_general | solution.py:52
  75.8 22.8 %all-to-all-done = bf16[128,4,8,128]{3,0,2,1:T(8,128)(2,1)S(1)} async-done(((bf16[128,4,8,128]{3,0,2,1:T(8,128)(2,1)}), bf16[128,4,8,128]{3,0,2,1:T(8,128)(2,1)S(1)}, u32[]{:S(2)}, u32[]{:S(2)}) %all-to-all-start) | async-done | bytes 1048608 | tf_op jit(solution)/shard_map/all_to_all | solution.py:109
  98.6 1.1 copy.27
  99.8 2.0 reduce_sum.69
  101.8 0.8 copy.22
  102.7 18.8 %all-gather.5.cloned.1.call-done = bf16[8,256,512]{2,1,0:T(8,128)(2,1)} async-done(((bf16[1,256,512]{2,1,0:T(8,128)(2,1)}), bf16[8,256,512]{2,1,0:T(8,128)(2,1)}) %all-gather.5.cloned.1.call-update) | async-done | bytes 2097168 | tf_op jit(solution)/shard_map/all_gather | solution.py:18
  121.5 2.0 reduce_sum.68
  123.5 0.8 copy.21
  124.3 26.7 %all-gather.9.cloned.1.call-done = bf16[8,256,512]{2,1,0:T(8,128)(2,1)} async-done(((bf16[1,256,512]{2,1,0:T(8,128)(2,1)}), bf16[8,256,512]{2,1,0:T(8,128)(2,1)}) %all-gather.9.cloned.1.call-update) | async-done | bytes 2097168 | tf_op jit(solution)/shard_map/all_gather | solution.py:18
  151.0 2.0 reduce_sum.70
  153.0 0.8 copy.23
  153.8 26.7 %all-gather.11.cloned.1.call-done = bf16[8,256,512]{2,1,0:T(8,128)(2,1)} async-done(((bf16[1,256,512]{2,1,0:T(8,128)(2,1)}), bf16[8,256,512]{2,1,0:T(8,128)(2,1)}) %all-gather.11.cloned.1.call-update) | async-done | bytes 2097168 | tf_op jit(solution)/shard_map/all_gather | solution.py:18
  180.6 2.0 reduce_sum.71
  182.5 0.9 copy.24
  183.4 2.2 pad_maximum_fusion
  185.6 18.3 %fusion.35 = (f32[512,8]{0,1:T(8,128)S(1)}, bf16[512,8,2048]{0,2,1:T(8,128)(2,1)}) fusion(pred[512,2048]{0,1:T(8,128)(4,1)} %compare_bitcast_fusion, bf16[512,8,128]{2,0,1:T(8,128)(2,1)S(1)} %bitcast.66, bf16[256,2048]{0,1:T(8,128)(2,1)} %pad_maximum_fusion), kind=kOutput, calls=%fused_computation.51 | convolution fusion | flops 4353689600 | bytes 22036480 | tf_op jit(solution)/shard_map/while/body/eval_jaxpr/sub | solution.py:59
  203.9 10.8 %fusion.14 = bf16[512,1,8,128]{3,0,2,1:T(8,128)(2,1)S(1)} fusion(bf16[512,8,2048]{0,2,1:T(8,128)(2,1)} %get-tuple-element.35, f32[512,8]{0,1:T(8,128)S(1)} %broadcast_maximum_fusion, bf16[256,2048]{0,1:T(8,128)(2,1)} %pad_maximum_fusion), kind=kOutput, calls=%fused_computation.15 | convolution fusion | flops 2148532224 | bytes 18366464 | tf_op jit(solution)/shard_map/while/body/eval_jaxpr/rnk,dk->rnd/dot_general | solution.py:61
  214.7 0.7 copy.30
  215.4 30.5 %all_to_all.30 = bf16[512,1,8,128]{3,2,1,0:T(8,128)(2,1)S(1)} all-to-all(bf16[512,1,8,128]{3,2,1,0:T(8,128)(2,1)S(1)} %copy.30), channel_id=1, replica_groups=mesh['ctx'=8,'head'=4] {'head'}, dimensions={0} | all-to-all | bytes 2097152 | tf_op jit(solution)/shard_map/all_to_all | solution.py:115
  245.9 0.2 copy.31
  246.1 1.3 reshape.183
  (9 shorter events, 0.0 us)
Async XLA Ops:
  6.5 1.6 copy-start
  6.5 7.6 %copy-start.2 = (s32[4]{0:T(128)S(1)}, s32[4]{0:T(128)}, u32[]{:S(2)}) copy-start(s32[4]{0:T(128)} %param.13) | copy-start | bytes 52
  6.5 56.0 %copy-start.3 = (f32[128]{0:T(128)S(1)}, f32[128]{0:T(128)}, u32[]{:S(2)}) copy-start(f32[128]{0:T(128)} %param.10) | copy-start | bytes 1540
  6.5 54.0 %reduce-scatter.2.cloned.1.call-start = ((), (), s32[]{:S(2)}) async-start(), calls=%async_computation.3 | async-start | bytes 2621440 | tf_op jit(solution)/shard_map/reduce_scatter | solution.py:82
  14.1 85.7 %all-gather.7.cloned.1.call-start = ((), (), s32[]{:S(2)}) async-start(), calls=%async_computation.5 | async-start | bytes 2359296 | tf_op jit(solution)/shard_map/all_gather | solution.py:18
  63.6 9.7 %copy-start.4 = (s32[512,4]{0,1:T(4,128)S(1)}, s32[512,4]{0,1:T(4,128)}, u32[]{:S(2)}) copy-start(s32[512,4]{0,1:T(4,128)} %param.11) | copy-start | bytes 24580
  63.6 9.7 %copy-start.5 = (s32[4]{0:T(128)S(1)}, s32[4]{0:T(128)}, u32[]{:S(2)}) copy-start(s32[4]{0:T(128)} %param.12) | copy-start | bytes 52
  64.6 56.9 %all-gather.5.cloned.1.call-start = ((), (), s32[]{:S(2)}) async-start(), calls=%async_computation.4 | async-start | bytes 2359296 | tf_op jit(solution)/shard_map/all_gather | solution.py:18
  65.4 85.7 %all-gather.9.cloned.1.call-start = ((), (), s32[]{:S(2)}) async-start(), calls=%async_computation.6 | async-start | bytes 2359296 | tf_op jit(solution)/shard_map/all_gather | solution.py:18
  65.9 114.6 %all-gather.11.cloned.1.call-start = ((), (), s32[]{:S(2)}) async-start(), calls=%async_computation.7 | async-start | bytes 2359296 | tf_op jit(solution)/shard_map/all_gather | solution.py:18
  69.5 29.1 %all-to-all-start = ((bf16[128,4,8,128]{3,0,2,1:T(8,128)(2,1)}), bf16[128,4,8,128]{3,0,2,1:T(8,128)(2,1)S(1)}, u32[]{:S(2)}, u32[]{:S(2)}) async-start(bf16[128,4,8,128]{3,0,2,1:T(8,128)(2,1)} %copy.26), calls=%async_computation.1 | async-start | bytes 2097152 | tf_op jit(solution)/shard_map/all_to_all | solution.py:109
  123.4 62.2 %copy-start.1 = (bf16[4,128,1,8,128]{4,1,0,3,2:T(8,128)(2,1)S(1)}, bf16[4,128,1,8,128]{4,1,0,3,2:T(8,128)(2,1)}, u32[]{:S(2)}) copy-start(bf16[4,128,1,8,128]{4,1,0,3,2:T(8,128)(2,1)} %copy.27) | copy-start | bytes 3145732
Sparse Core Ops, SparseCore 0:
  14.2 46.3 reduce-scatter.1
  64.7 26.9 all-gather.6
  93.7 27.7 all-gather.4
  123.2 27.7 all-gather.8
  152.8 27.7 all-gather.10
